TPU v7x, 512 devices: a whole 4x8x8 slice. The times are simulated.
512 devices in a mesh: span: 4 (over x), seq: 32 (over z_hi, y, core), head: 4 (over z_lo).
Axes of the slice: x: 4, y: 8, z: 8 (z_hi: 2, z_lo: 4; z = z_hi * 4 + z_lo), core: 2. Of those that a mesh axis runs over, the one named last changes fastest.
Arguments:
- query_proj: bfloat16 [4, 1280, 3072], P('span', 'seq', 'head'), may hold values from -12 to 12
- key_proj: bfloat16 [4, 1280, 3072], P('span', 'seq', 'head'), may hold values from -12 to 12
- value_proj: bfloat16 [4, 1280, 3072], P('span', 'seq', 'head'), may hold values from -24 to 24
- block_order: int32 [4], replicated, may hold values from 0 to 3, each once
- valid_frames: int32 [4], replicated, may hold values from 1 to 8, as said below
- noise_steps: int32 [4], replicated, may hold values from 0 to 3
- gate_table: float32 [4, 6144], P(None, 'seq'), may hold values from 1 to 10
- out_weight: bfloat16 [3072, 6144], P('head', 'seq'), may hold values from -0.109375 to 0.109375
- residual: bfloat16 [4, 1280, 6144], P('span', 'head', 'seq'), may hold values from -3 to 3
Outputs:
- mixed: bfloat16 [4, 1280, 6144], P('span', 'head', 'seq')
Inputs may be any that keep to these rules, and one draw needn't show every extreme that they name: `valid_frames`: some block has all 8 frames open.
All inputs are finite; a program needn't handle non-finite values.
Results may differ from a plain program's by a relative error of at most 0.017.
Values may be sent and summed in bfloat16 or wider, within the bound.
No kernel may reach another device: no remote copies, remote signals or barrier semaphores. Data moves between devices by JAX's collectives and lax.ppermute only.
A program may use at most 128 MiB of HBM per device.

v0:
```python
import jax
import jax.numpy as jnp
from jax import lax
from jax.sharding import PartitionSpec as P

HD = 128
FRAMES = 8
floor_score = -1e30


def lookup(entries, picked):
    slots = jnp.arange(entries.shape[0], dtype=jnp.int32)
    return jnp.sum(jnp.where(slots[None, :] == picked[:, None], entries[None, :], 0), axis=1)


def attend(carry_state, queries, keys_piece, values_piece, visible):
    running_max, denominator, summed = carry_state
    score_scale = 1.0 / queries.shape[-1] ** 0.5
    scores = (
        jnp.einsum("qhe,khe->hqk", queries, keys_piece, preferred_element_type=jnp.float32)
        * score_scale
    )
    scores = jnp.where(visible[None, None, :], scores, floor_score)
    new_max = jnp.maximum(running_max, jnp.max(scores, axis=2))
    weights = jnp.where(visible[None, None, :], jnp.exp(scores - new_max[:, :, None]), 0.0)
    denominator = jnp.sum(weights, axis=2)
    summed = jnp.einsum(
        "hqk,khe->hqe",
        weights.astype(jnp.bfloat16),
        values_piece,
        preferred_element_type=jnp.float32,
    )
    return (new_max, denominator, summed)


def attend_some(carry_state, queries, keys_piece, values_piece, visible):
    return attend(carry_state, queries, keys_piece, values_piece, visible)


def shards(
    query_proj,
    key_proj,
    value_proj,
    block_order,
    valid_frames,
    noise_steps,
    gate_table,
    out_weight,
    residual,
):
    head_dim = HD
    tokens_here = query_proj.shape[1]
    block_len = tokens_here * lax.axis_size("seq")
    frame_len = block_len // FRAMES
    heads_here = query_proj.shape[2] // head_dim
    block_here = lax.axis_index("span")
    order_here = lookup(block_order, jnp.full((1,), block_here, jnp.int32))[0]
    queries = query_proj[0].reshape(tokens_here, heads_here, head_dim)
    start_state = (
        jnp.full((heads_here, tokens_here), floor_score, jnp.float32),
        jnp.zeros((heads_here, tokens_here), jnp.float32),
        jnp.zeros((heads_here, tokens_here, head_dim), jnp.float32),
    )
    keys_piece = lax.all_gather(key_proj, ("span", "seq"), axis=1, tiled=True)
    values_piece = lax.all_gather(value_proj, ("span", "seq"), axis=1, tiled=True)
    count_rows = keys_piece.shape[1]
    positions = jnp.arange(count_rows, dtype=jnp.int32)
    owners = positions // block_len
    frame_index = positions % block_len // frame_len
    visible = (lookup(block_order, owners) <= order_here) & (
        frame_index < lookup(valid_frames, owners)
    )
    final_state = attend_some(
        start_state,
        queries,
        keys_piece[0].reshape(count_rows, heads_here, head_dim),
        values_piece[0].reshape(count_rows, heads_here, head_dim),
        visible,
    )
    running_max, denominator, summed = final_state
    attended = (
        (summed / denominator[:, :, None])
        .transpose(1, 0, 2)
        .reshape(tokens_here, heads_here * head_dim)
        .astype(jnp.bfloat16)
    )
    partial_sums = jnp.dot(
        lax.all_gather(attended, "seq", axis=0, tiled=True),
        out_weight,
        preferred_element_type=jnp.float32,
    )
    head_total = lax.psum_scatter(
        partial_sums.astype(jnp.bfloat16), "head", scatter_dimension=0, tiled=True
    ).astype(jnp.float32)
    step_here = lookup(noise_steps, jnp.full((1,), block_here, jnp.int32))[0]
    step_slots = jnp.arange(gate_table.shape[0], dtype=jnp.int32)
    gate_row = jnp.sum(jnp.where((step_slots == step_here)[:, None], gate_table, 0.0), axis=0)
    mixed = (residual[0].astype(jnp.float32) + gate_row[None, :] * head_total).astype(jnp.bfloat16)
    return mixed[None]


def solution(mesh):
    placed = (
        P("span", "seq", "head"),
        P("span", "seq", "head"),
        P("span", "seq", "head"),
        P(),
        P(),
        P(),
        P(None, "seq"),
        P("head", "seq"),
        P("span", "head", "seq"),
    )
    return jax.shard_map(
        shards, mesh=mesh, in_specs=placed, out_specs=P("span", "head", "seq"), check_vma=False
    )
```

profile of v0, /device:TPU:2, one launch (start us, length us, event | category | flops | bytes accessed | tf_op | source)
XLA Modules:
  0.0 468.5 jit_solution(13273609546740067536)
XLA Ops:
  6.5 0.0 copy-start
  6.5 0.0 all-gather.4.cloned.1.call-start
  6.5 0.7 all-gather.4.cloned.1.call-update
  7.3 0.0 all-gather.6.cloned.1.call-start
  7.3 0.7 all-gather.6.cloned.1.call-update
  8.0 0.0 all-gather.8.cloned.1.call-start
  8.1 0.9 reshape_squeeze.9
  9.0 1.3 fusion.38
  10.3 0.8 select_reduce_fusion
  11.1 0.7 compare_and_fusion
  11.8 161.0 %all-gather.4.cloned.1.call-done = bf16[1,5120,768]{2,1,0:T(8,128)(2,1)} async-done(((bf16[1,40,768]{2,1,0:T(8,128)(2,1)}), bf16[1,5120,768]{2,1,0:T(8,128)(2,1)}) %all-gather.4.cloned.1.call-update) | async-done | bytes 7864336 | tf_op jit(solution)/shard_map/all_gather | solution.py:64
  172.9 10.7 %copy.23 = bf16[1,5120,768]{1,2,0:T(8,128)(2,1)} copy(bf16[1,5120,768]{2,1,0:T(8,128)(2,1)} %all-gather.4.cloned.1.call-done) | data formatting | bytes 15728640 | tf_op jit(solution)/shard_map/all_gather | solution.py:64
  183.6 4.8 %fusion.40 = (f32[6,40]{1,0:T(8,128)S(1)}, f32[6,40,5120]{2,1,0:T(8,128)S(1)}) fusion(bf16[5120,6,128]{0,2,1:T(8,128)(2,1)} %bitcast.27, bf16[40,6,128]{2,1,0:T(8,128)(2,1)S(1)} %reshape_squeeze.9, pred[5120]{0:T(1024)(128)(4,1)S(1)} %compare_and_fusion), kind=kOutput, calls=%fused_computation.50 | convolution fusion | flops 318258944 | bytes 12847040 | tf_op jit(solution)/shard_map/qhe,khe->hqk/dot_general | solution.py:20
  188.4 0.0 copy-start.1
  188.4 2.2 copy-done.1
  190.6 1.1 fusion.1
  191.7 135.4 %all-gather.6.cloned.1.call-done = bf16[1,5120,768]{2,1,0:T(8,128)(2,1)} async-done(((bf16[1,40,768]{2,1,0:T(8,128)(2,1)}), bf16[1,5120,768]{2,1,0:T(8,128)(2,1)}) %all-gather.6.cloned.1.call-update) | async-done | bytes 7864336 | tf_op jit(solution)/shard_map/all_gather | solution.py:65
  327.1 10.4 %copy.26 = bf16[1,5120,768]{1,2,0:T(8,128)(2,1)} copy(bf16[1,5120,768]{2,1,0:T(8,128)(2,1)} %all-gather.6.cloned.1.call-done) | data formatting | bytes 15728640 | tf_op jit(solution)/shard_map/all_gather | solution.py:65
  337.5 0.0 copy-start.4
  337.5 0.0 copy-start.3
  337.5 7.7 %fusion.17 = bf16[6,5,8,128]{3,2,1,0:T(8,128)(2,1)S(1)} fusion(bf16[5120,6,128]{0,2,1:T(8,128)(2,1)} %bitcast.26, f32[6,40,5120]{2,1,0:T(8,128)} %copy-done.1, f32[6,40]{1,0:T(8,128)S(1)} %broadcast_maximum_fusion, pred[5120]{0:T(1024)(128)(4,1)S(1)} %compare_and_fusion, f32[40,6]{0,1:T(8,128)S(1)} %bitcast.29), kind=kOutput, calls=%fused_computation.13 | convolution fusion | flops 318320640 | bytes 12848000 | tf_op jit(solution)/shard_map/hqk,khe->hqe/dot_general | solution.py:27
  345.1 0.0 copy-start.2
  345.2 0.6 copy.39
  345.8 0.0 all-gather.8.cloned.1.call-update
  345.8 0.0 reduce-scatter.4.cloned.1.call-start
  345.9 86.9 %all-gather.8.cloned.1.call-done = bf16[1280,768]{1,0:T(8,128)(2,1)} async-done(((bf16[40,768]{1,0:T(8,128)(2,1)}), bf16[1280,768]{1,0:T(8,128)(2,1)}) %all-gather.8.cloned.1.call-update) | async-done | bytes 1966096 | tf_op jit(solution)/shard_map/all_gather | solution.py:88
  432.7 0.0 copy-done
  432.7 2.3 convolution_convert_fusion
  435.1 1.1 copy.31
  436.1 0.0 reduce-scatter.4.cloned.1.call-update
  436.2 0.0 copy-done.4
  436.2 0.6 fusion.37
  436.8 0.6 iota_compare_fusion.1
  437.5 0.0 copy-done.3
  437.5 0.1 select_reduce_fusion.2
  437.6 22.5 %reduce-scatter.4.cloned.1.call-done = bf16[320,192]{1,0:T(8,128)(2,1)} async-done(((bf16[1280,192]{1,0:T(8,128)(2,1)}), bf16[320,192]{1,0:T(8,128)(2,1)}) %reduce-scatter.4.cloned.1.call-update) | async-done | bytes 122896
  460.1 1.1 copy.32
  461.2 0.0 copy-done.2
  461.2 0.8 fusion.21
  (2 shorter events, 0.0 us)
Async XLA Ops:
  6.5 426.2 %copy-start = (bf16[768,192]{0,1:T(8,128)(2,1)S(1)}, bf16[768,192]{0,1:T(8,128)(2,1)}, u32[]{:S(2)}) copy-start(bf16[768,192]{0,1:T(8,128)(2,1)} %param.16) | copy-start | bytes 884740
  6.5 166.3 %all-gather.4.cloned.1.call-start = ((), (), s32[]{:S(2)}) async-start(), calls=%async_computation.1 | async-start | bytes 7925760 | tf_op jit(solution)/shard_map/all_gather | solution.py:64
  7.3 319.8 %all-gather.6.cloned.1.call-start = ((), (), s32[]{:S(2)}) async-start(), calls=%async_computation.2 | async-start | bytes 7925760 | tf_op jit(solution)/shard_map/all_gather | solution.py:65
  8.0 424.7 %all-gather.8.cloned.1.call-start = ((), (), s32[]{:S(2)}) async-start(), calls=%async_computation.3 | async-start | bytes 2027520 | tf_op jit(solution)/shard_map/all_gather | solution.py:88
  188.4 2.2 copy-start.1
  337.5 98.7 %copy-start.4 = (s32[4]{0:T(128)S(1)}, s32[4]{0:T(128)}, u32[]{:S(2)}) copy-start(s32[4]{0:T(128)} %param.14) | copy-start | bytes 52
  337.5 100.0 %copy-start.3 = (f32[4,192]{1,0:T(4,128)S(1)}, f32[4,192]{1,0:T(4,128)}, u32[]{:S(2)}) copy-start(f32[4,192]{1,0:T(4,128)} %param.15) | copy-start | bytes 9220
  345.1 116.0 %copy-start.2 = (bf16[1,320,192]{1,2,0:T(8,128)(2,1)S(1)}, bf16[1,320,192]{1,2,0:T(8,128)(2,1)}, u32[]{:S(2)}) copy-start(bf16[1,320,192]{1,2,0:T(8,128)(2,1)} %param.17) | copy-start | bytes 368644
  345.8 114.3 %reduce-scatter.4.cloned.1.call-start = ((), (), s32[]{:S(2)}) async-start(), calls=%async_computation.4 | async-start | bytes 819200
Sparse Core Ops, SparseCore 0:
  12.0 160.8 all-gather.3
  177.5 149.5 all-gather.5
  345.9 86.7 all-gather.7
  436.3 23.7 reduce-scatter.3
where the time goes:
time: 469 us; the launch traced here: 468 us
  waiting for transfers between devices  407 us (87%)
  local copies, waits for them, and re-layouts  27 us (6%)
  matrix products  14.8 us (3%)
  between operations  13.2 us (3%)
  other arithmetic  6.04 us (1%)
    all_gather x1, waiting for transfers between devices, shards(): keys_piece = lax.all_gather(key_proj, ('span', 'seq'), axis=1, tiled=True)  161 us
    all_gather x1, waiting for transfers between devices, shards(): lax.all_gather(value_proj, ('span', 'seq'), axis=1, tiled=True)  135 us
    all_gather x1, waiting for transfers between devices, shards(): lax.all_gather(attended, 'seq', axis=0, tiled=True)  86.9 us
    unnamed x5, waiting for transfers between devices  24 us
    all_gather x1, local copies, waits for them, and re-layouts, shards(): keys_piece = lax.all_gather(key_proj, ('span', 'seq'), axis=1, tiled=True)  10.7 us
    all_gather x1, local copies, waits for them, and re-layouts, shards(): lax.all_gather(value_proj, ('span', 'seq'), axis=1, tiled=True)  10.4 us
  transfers between devices with their start and end apart: 4, of which 4 were waited for; matrix products, arithmetic and copies ran while one was open for 5% of the time, Pallas kernels for 0%

commit v1 on v0

--- a/solution.py
+++ b/solution.py
@@ -85,7 +85,9 @@
         .astype(jnp.bfloat16)
     )
     partial_sums = jnp.dot(
-        lax.all_gather(attended, "seq", axis=0, tiled=True),
+        jnp.concatenate(
+            lax.all_to_all(jnp.stack([attended] * lax.axis_size("seq")), "seq", 0, 0), axis=0
+        ),
         out_weight,
         preferred_element_type=jnp.float32,
     )

time: 469 us -> 438 us (0.934)
  waiting for transfers between devices: 407 us -> 321 us
  blocking collectives: 0 us -> 56.6 us
    all_gather x1 -> x0, waiting for transfers between devices: 86.9 us -> none  [shards(): lax.all_gather(attended, 'seq', axis=0, tiled=True)]
    all_to_all x0 -> x1, blocking collectives: none -> 56.6 us  [shards(): lax.all_to_all(jnp.stack([attended] * lax.axis_size('seq')), 'seq', 0, 0)]
    unnamed x5 -> x4, waiting for transfers between devices: 24 us -> 24.6 us
  transfers between devices with their start and end apart: 4 -> 3, of which waited for: 4 -> 3; matrix products, arithmetic and copies ran while one was open for 5% -> 5% of each run, Pallas kernels for 0% -> 0%
where the time goes in v1:
time: 438 us; the launch traced here: 437 us
  waiting for transfers between devices  321 us (73%)
  blocking collectives  56.6 us (13%)
  local copies, waits for them, and re-layouts  26.5 us (6%)
  matrix products  13.3 us (3%)
  between operations  13.2 us (3%)
  other arithmetic  6.04 us (1%)
    all_gather x1, waiting for transfers between devices, shards(): keys_piece = lax.all_gather(key_proj, ('span', 'seq'), axis=1, tiled=True)  161 us
    all_gather x1, waiting for transfers between devices, shards(): lax.all_gather(value_proj, ('span', 'seq'), axis=1, tiled=True)  135 us
    all_to_all x1, blocking collectives, shards(): lax.all_to_all(jnp.stack([attended] * lax.axis_size('seq')), 'seq', 0, 0)  56.6 us
    unnamed x4, waiting for transfers between devices  24.6 us
    all_gather x1, local copies, waits for them, and re-layouts, shards(): keys_piece = lax.all_gather(key_proj, ('span', 'seq'), axis=1, tiled=True)  10.7 us
    all_gather x1, local copies, waits for them, and re-layouts, shards(): lax.all_gather(value_proj, ('span', 'seq'), axis=1, tiled=True)  10.4 us
  transfers between devices with their start and end apart: 3, of which 3 were waited for; matrix products, arithmetic and copies ran while one was open for 5% of the time, Pallas kernels for 0%

profile of v1, /device:TPU:2, one launch (start us, length us, event | category | flops | bytes accessed | tf_op | source)
XLA Modules:
  0.0 436.8 jit_solution(17486755455761690828)
XLA Ops:
  6.5 0.0 copy-start
  6.5 0.0 all-gather.3.cloned.1.call-start
  6.5 0.7 all-gather.3.cloned.1.call-update
  7.3 0.0 all-gather.5.cloned.1.call-start
  7.3 0.7 all-gather.5.cloned.1.call-update
  8.0 0.0 reduce-scatter.4.cloned.1.call-start
  8.1 0.9 reshape_squeeze.9
  9.0 1.3 fusion.38
  10.3 0.8 select_reduce_fusion
  11.1 0.7 compare_and_fusion
  11.8 161.0 %all-gather.3.cloned.1.call-done = bf16[1,5120,768]{2,1,0:T(8,128)(2,1)} async-done(((bf16[1,40,768]{2,1,0:T(8,128)(2,1)}), bf16[1,5120,768]{2,1,0:T(8,128)(2,1)}) %all-gather.3.cloned.1.call-update) | async-done | bytes 7864336 | tf_op jit(solution)/shard_map/all_gather | solution.py:64
  172.9 10.7 %copy.23 = bf16[1,5120,768]{1,2,0:T(8,128)(2,1)} copy(bf16[1,5120,768]{2,1,0:T(8,128)(2,1)} %all-gather.3.cloned.1.call-done) | data formatting | bytes 15728640 | tf_op jit(solution)/shard_map/all_gather | solution.py:64
  183.6 4.8 %fusion.40 = (f32[6,40]{1,0:T(8,128)S(1)}, f32[6,40,5120]{2,1,0:T(8,128)S(1)}) fusion(bf16[5120,6,128]{0,2,1:T(8,128)(2,1)} %bitcast.28, bf16[40,6,128]{2,1,0:T(8,128)(2,1)S(1)} %reshape_squeeze.9, pred[5120]{0:T(1024)(128)(4,1)S(1)} %compare_and_fusion), kind=kOutput, calls=%fused_computation.50 | convolution fusion | flops 318258944 | bytes 12847040 | tf_op jit(solution)/shard_map/qhe,khe->hqk/dot_general | solution.py:20
  188.4 0.0 copy-start.1
  188.4 2.2 copy-done.1
  190.6 1.1 fusion.1
  191.7 135.4 %all-gather.5.cloned.1.call-done = bf16[1,5120,768]{2,1,0:T(8,128)(2,1)} async-done(((bf16[1,40,768]{2,1,0:T(8,128)(2,1)}), bf16[1,5120,768]{2,1,0:T(8,128)(2,1)}) %all-gather.5.cloned.1.call-update) | async-done | bytes 7864336 | tf_op jit(solution)/shard_map/all_gather | solution.py:65
  327.1 10.4 %copy.26 = bf16[1,5120,768]{1,2,0:T(8,128)(2,1)} copy(bf16[1,5120,768]{2,1,0:T(8,128)(2,1)} %all-gather.5.cloned.1.call-done) | data formatting | bytes 15728640 | tf_op jit(solution)/shard_map/all_gather | solution.py:65
  337.5 7.6 %fusion.17 = bf16[6,5,8,128]{3,2,1,0:T(8,128)(2,1)S(1)} fusion(bf16[5120,6,128]{0,2,1:T(8,128)(2,1)} %bitcast.27, f32[6,40,5120]{2,1,0:T(8,128)} %copy-done.1, f32[6,40]{1,0:T(8,128)S(1)} %broadcast_maximum_fusion, pred[5120]{0:T(1024)(128)(4,1)S(1)} %compare_and_fusion, f32[40,6]{0,1:T(8,128)S(1)} %bitcast.31), kind=kOutput, calls=%fused_computation.13 | convolution fusion | flops 318320640 | bytes 12848000 | tf_op jit(solution)/shard_map/hqk,khe->hqe/dot_general | solution.py:27
  345.1 0.0 copy-start.4
  345.1 0.0 copy-start.3
  345.2 0.1 stack.2
  345.3 0.0 copy-start.2
  345.3 56.6 %all_to_all.5 = bf16[32,40,768]{2,1,0:T(8,128)(2,1)S(1)} all-to-all(bf16[32,40,768]{2,1,0:T(8,128)(2,1)S(1)} %stack.2), channel_id=1, replica_groups=mesh['span'=4,'seq'=32,'head'=4] {'seq'}, dimensions={0} | all-to-all | bytes 3932160 | tf_op jit(solution)/shard_map/all_to_all | solution.py:89
  401.9 0.0 copy-done
  401.9 0.8 convolution_convert_fusion
  402.7 1.1 copy.31
  403.8 0.0 reduce-scatter.4.cloned.1.call-update
  403.8 0.0 copy-done.4
  403.8 0.6 fusion.37
  404.5 0.6 iota_compare_fusion.1
  405.1 0.0 copy-done.3
  405.1 0.1 select_reduce_fusion.2
  405.2 23.2 %reduce-scatter.4.cloned.1.call-done = bf16[320,192]{1,0:T(8,128)(2,1)} async-done(((bf16[1280,192]{1,0:T(8,128)(2,1)}), bf16[320,192]{1,0:T(8,128)(2,1)}) %reduce-scatter.4.cloned.1.call-update) | async-done | bytes 122896
  428.4 1.1 copy.32
  429.5 0.0 copy-done.2
  429.5 0.8 fusion.21
  (3 shorter events, 0.0 us)
Async XLA Ops:
  6.5 395.4 %copy-start = (bf16[768,192]{0,1:T(8,128)(2,1)S(1)}, bf16[768,192]{0,1:T(8,128)(2,1)}, u32[]{:S(2)}) copy-start(bf16[768,192]{0,1:T(8,128)(2,1)} %param.16) | copy-start | bytes 884740
  6.5 166.3 %all-gather.3.cloned.1.call-start = ((), (), s32[]{:S(2)}) async-start(), calls=%async_computation.2 | async-start | bytes 7925760 | tf_op jit(solution)/shard_map/all_gather | solution.py:64
  7.3 319.8 %all-gather.5.cloned.1.call-start = ((), (), s32[]{:S(2)}) async-start(), calls=%async_computation.3 | async-start | bytes 7925760 | tf_op jit(solution)/shard_map/all_gather | solution.py:65
  8.0 420.4 %reduce-scatter.4.cloned.1.call-start = ((), (), s32[]{:S(2)}) async-start(), calls=%async_computation.4 | async-start | bytes 819200
  188.4 2.2 copy-start.1
  345.1 58.7 %copy-start.4 = (s32[4]{0:T(128)S(1)}, s32[4]{0:T(128)}, u32[]{:S(2)}) copy-start(s32[4]{0:T(128)} %param.14) | copy-start | bytes 52
  345.1 60.0 %copy-start.3 = (f32[4,192]{1,0:T(4,128)S(1)}, f32[4,192]{1,0:T(4,128)}, u32[]{:S(2)}) copy-start(f32[4,192]{1,0:T(4,128)} %param.15) | copy-start | bytes 9220
  345.3 84.2 %copy-start.2 = (bf16[1,320,192]{1,2,0:T(8,128)(2,1)S(1)}, bf16[1,320,192]{1,2,0:T(8,128)(2,1)}, u32[]{:S(2)}) copy-start(bf16[1,320,192]{1,2,0:T(8,128)(2,1)} %param.17) | copy-start | bytes 368644
Sparse Core Ops, SparseCore 0:
  12.0 160.8 all-gather.2
  177.5 149.5 all-gather.4
  403.9 24.4 reduce-scatter.3
